TPU v7x, 256 devices: a whole 4x4x8 slice. The times are simulated.
256 devices in a mesh: sec: 4 (over x_lo, core), dom: 64 (over y, x_hi, z).
Axes of the slice: x: 4 (x_hi: 2, x_lo: 2; x = x_hi * 2 + x_lo), y: 4, z: 8, core: 2. Of those that a mesh axis runs over, the one named last changes fastest.
Arguments:
- state: float32 [4, 64, 393216], P('sec', None, 'dom'), may hold values from -6 to 6
- send_list: int32 [4, 64, 2, 12], P('sec', 'dom'), may hold values from 0 to 47
- op_index: int32 [4, 3072, 3], P('sec', 'dom'), may hold values from 0 to 71, as said below
- op_weight: float32 [4, 3072, 3, 128, 128], P('sec', 'dom'), may hold values from -0.3125 to 0.3125
- vertical: float32 [4, 64, 64], P('sec'), may hold values from -0.75 to 0.75
- flux_weight: float32 [4, 16, 16], P('sec'), may hold values from -1.5 to 1.5
- remap_index: int32 [3072, 2], P('dom'), may hold values from 0 to 215, as said below
- remap_weight: float32 [3072, 2, 128, 128], P('dom'), may hold values from -0.375 to 0.375
- wet_mask: int32 [393216], P('dom'), may hold values 0 or 1
Outputs:
- state_out: float32 [4, 64, 393216], P('sec', None, 'dom')
Inputs may be any that keep to these rules, and one draw needn't show every extreme that they name: `op_index`: indices into a partition's block list E: its 48 own blocks, then 12 from the previous partition, then 12 from the next. `remap_index`: indices into an ocean partition's candidate list of 216 flux blocks.
All inputs are finite; a program needn't handle non-finite values. No bound on the sum of `wet_mask` on one device may be relied on, other than what follows from the above.
Results may differ from a plain program's by a relative error of at most 0.0001.
Values sent between devices are 32-bit elements; how exact they have to be, the bound alone decides.
A program may use at most 128 MiB of HBM per device.

v0:
```python
import jax
import jax.numpy as jnp
from jax import lax
from jax.sharding import PartitionSpec as P

STEPS = 2


def extended_2(x, sides, width):
    for axis, dim in sides:
        size, length = (lax.axis_size(axis), x.shape[dim])
        up = [(i, (i + 1) % size) for i in range(size)]
        down = [(j, i) for i, j in up]
        last = lax.slice_in_dim(x, length - width, length, axis=dim)
        initial = lax.slice_in_dim(x, 0, width, axis=dim)
        before = lax.ppermute(last, axis, up)
        after = lax.ppermute(initial, axis, down)
        x = jnp.concatenate([before, x, after], axis=dim)
    return x


def apply_operator(column_state, send_rows, pattern, weights, block_size, edge_count):
    levels, slot_count = column_state.shape
    blocks = column_state.reshape(levels, -1, block_size)
    block_count = blocks.shape[1]
    rim_width = edge_count * block_size
    outgoing = blocks[:, send_rows, :].reshape(levels, 2 * rim_width)
    extended = extended_2(outgoing, (("dom", 1),), rim_width)
    from_left = extended[:, :rim_width]
    from_right = extended[:, extended.shape[1] - rim_width :]
    everything = jnp.concatenate(
        [
            blocks,
            from_left.reshape(levels, edge_count, block_size),
            from_right.reshape(levels, edge_count, block_size),
        ],
        axis=1,
    )
    picked = everything[:, pattern, :].reshape(levels, block_count, -1, block_size)
    result = jnp.einsum("lnkb,nkbc->lnc", picked, weights, precision=lax.Precision.HIGHEST)
    return column_state + result.reshape(levels, slot_count)


def local(
    state,
    send_list,
    op_index,
    op_weight,
    vertical,
    flux_weight,
    remap_index,
    remap_weight,
    wet_mask,
):
    levels = state.shape[1]
    slot_count = state.shape[2]
    block_size = op_weight.shape[3]
    block_count = slot_count // block_size
    edge_count = send_list.shape[3]
    atm_cols = slot_count // 2
    atm_blocks = block_count // 2
    flux_rows = flux_weight.shape[1]
    surf_levels = flux_rows // 2
    remap_count = remap_index.shape[1]
    is_ocean = lax.axis_index("sec") == lax.axis_size("sec") - 1
    send_rows = send_list[0, 0].reshape(-1)
    pattern = op_index[0].reshape(-1)
    weights = op_weight[0]
    vertical_matrix = vertical[0]
    flux_matrix = flux_weight[0]
    wet_columns = wet_mask.astype(jnp.float32)[None, :]
    source_rows = remap_index.reshape(-1)
    column_state = state[0]
    for counter in range(STEPS):
        updated = apply_operator(column_state, send_rows, pattern, weights, block_size, edge_count)
        mixed_field = jnp.dot(vertical_matrix, updated, precision=lax.Precision.HIGHEST)
        surface = jnp.concatenate(
            [
                mixed_field[levels - surf_levels :, :atm_cols],
                mixed_field[levels - surf_levels :, atm_cols:],
            ],
            axis=0,
        )
        surface_flux = jnp.tanh(jnp.dot(flux_matrix, surface, precision=lax.Precision.HIGHEST))
        sections = lax.all_gather(surface_flux[None], "sec", axis=0, tiled=True)
        atmosphere = sections[: sections.shape[0] - 1]
        nearby = extended_2(atmosphere[None], (("dom", 0),), 1)
        candidates = nearby.reshape(3, 3, flux_rows, atm_blocks, block_size).transpose(
            0, 1, 3, 2, 4
        )
        candidates = candidates.reshape(9 * atm_blocks, flux_rows, block_size)
        chosen = candidates[source_rows].reshape(block_count, remap_count, flux_rows, block_size)
        forcing = jnp.einsum(
            "nrfb,nrbc->fnc", chosen, remap_weight, precision=lax.Precision.HIGHEST
        )
        forcing = forcing.reshape(flux_rows, slot_count)
        ocean_field = wet_columns * (
            mixed_field + jnp.pad(forcing, ((0, levels - flux_rows), (0, 0)))
        )
        column_state = jnp.where(is_ocean, ocean_field, mixed_field)
    return column_state[None]


def solution(mesh):
    in_specs = (
        P("sec", None, "dom"),
        P("sec", "dom", None, None),
        P("sec", "dom", None),
        P("sec", "dom", None, None, None),
        P("sec", None, None),
        P("sec", None, None),
        P("dom", None),
        P("dom", None, None, None),
        P("dom"),
    )
    out_specs = P("sec", None, "dom")
    return jax.shard_map(local, mesh=mesh, in_specs=in_specs, out_specs=out_specs, check_vma=False)
```

profile of v0, /device:TPU:3, one launch (start us, length us, event | category | flops | bytes accessed | tf_op | source)
XLA Modules:
  0.0 180.2 jit_solution(14282391342886841137)
XLA Ops:
  0.0 0.8 reshape_squeeze.10
  0.8 1.7 copy.68
  2.5 0.5 copy.32
  3.0 0.0 copy-start.3
  3.0 0.6 gather_fusion
  3.6 0.0 copy-start.12
  3.6 0.1 copy_bitcast_fusion.2
  3.7 0.1 fusion.36
  3.7 0.4 copy-done.3
  4.1 1.6 collective-permute-start
  5.8 8.0 %collective-permute-start.1 = (f32[64,1536]{1,0:T(8,128)S(1)}, f32[64,1536]{1,0:T(8,128)S(1)}, u32[]{:S(2)}, u32[]{:S(2)}) collective-permute-start(f32[64,1536]{1,0:T(8,128)S(1)} %get-tuple-element.16), channel_id=1, source_target_pairs={{1,0},{2,1},{3,2},{4,3},{5,4},{6,5},{7,6},{8,7},{9,8},{10,9},{11,1... | collective-permute-start | bytes 1179656 | tf_op jit(solution)/shard_map/ppermute | solution.py:17
  13.7 0.1 copy.35
  13.8 0.1 reshape_squeeze.11
  13.9 0.0 copy-start.4
  14.0 8.6 %collective-permute-done = f32[64,1536]{1,0:T(8,128)S(1)} collective-permute-done((f32[64,1536]{1,0:T(8,128)S(1)}, f32[64,1536]{1,0:T(8,128)S(1)}, u32[]{:S(2)}, u32[]{:S(2)}) %collective-permute-start) | collective-permute-done | bytes 393248 | tf_op jit(solution)/shard_map/ppermute | solution.py:16
  22.7 0.3 pad_maximum_fusion
  22.9 3.0 %gather_fusion.1 = f32[144,64,128]{2,1,0:T(8,128)} fusion(f32[64,72,128]{2,0,1:T(8,128)S(1)} %pad_maximum_fusion, s32[1024]{0:T(1024)S(1)} %pad_clamp_fusion.1), kind=kCustom, calls=%fused_computation.1 | custom fusion | bytes 9437760 | tf_op jit(solution)/shard_map/gather | solution.py:39
  25.9 9.7 %fusion.9 = f32[64,48,128]{2,0,1:T(8,128)S(1)} fusion(f32[64,48,3,128]{3,0,2,1:T(8,128)} %bitcast.148, f32[1,48,3,128,128]{4,3,2,1,0:T(8,128)} %param.12), kind=kOutput, calls=%fused_computation.27 | convolution fusion | flops 1811939328 | bytes 15728640 | tf_op jit(solution)/shard_map/lnkb,nkbc->lnc/dot_general | solution.py:40
  35.7 0.9 copy.36
  36.6 0.0 copy-start.7
  36.6 1.4 reshape.155
  38.0 0.5 copy-done.7
  38.6 3.0 %convolution_bitcast_fusion.1 = f32[64,6144]{1,0:T(8,128)S(1)} fusion(f32[1,64,6144]{2,1,0:T(8,128)S(1)} %copy-done.7, f32[1,64,6144]{2,1,0:T(8,128)} %reshape.155, f32[1,64,64]{2,1,0:T(8,128)S(1)} %copy-done), kind=kOutput, calls=%fused_computation.11 | convolution fusion | flops 302383104 | bytes 4734976 | tf_op jit(solution)/shard_map/dot_general | solution.py:76
  41.6 0.3 fusion.5
  41.9 0.0 copy-start.11
  42.0 0.0 copy-start.13
  42.0 9.7 %all-gather = f32[64,3072]{1,0:T(8,128)S(1)} all-gather(f32[16,3072]{1,0:T(8,128)S(1)} %fusion.5), channel_id=2, replica_groups=mesh['sec'=4,'dom'=64] {'sec'}, dimensions={0}, use_global_device_ids=true | all-gather | bytes 983040 | tf_op jit(solution)/shard_map/all_gather | solution.py:85
  51.7 0.1 slice_bitcast_fusion.1
  51.8 1.4 copy.37
  53.2 6.5 %collective-permute-start.3 = (f32[1,3,16,3072]{3,0,2,1:T(1,128)}, f32[1,3,16,3072]{3,0,2,1:T(1,128)S(1)}, u32[]{:S(2)}, u32[]{:S(2)}) collective-permute-start(f32[1,3,16,3072]{3,0,2,1:T(1,128)} %copy.37), channel_id=1, source_target_pairs={{1,0},{2,1},{3,2},{4,3},{5,4},{6,5},{7,6},{8,7},{9,8},{10,9},{11,1... | collective-permute-start | bytes 1769480 | tf_op jit(solution)/shard_map/ppermute | solution.py:17
  59.8 0.1 copy.41
  59.9 0.1 reshape.157
  60.0 0.1 copy.69
  60.1 12.5 %collective-permute-done.3 = f32[1,3,16,3072]{3,0,2,1:T(1,128)S(1)} collective-permute-done((f32[1,3,16,3072]{3,0,2,1:T(1,128)}, f32[1,3,16,3072]{3,0,2,1:T(1,128)S(1)}, u32[]{:S(2)}, u32[]{:S(2)}) %collective-permute-start.3) | collective-permute-done | bytes 589856 | tf_op jit(solution)/shard_map/ppermute | solution.py:17
  72.6 7.5 %collective-permute-done.2 = f32[1,3,16,3072]{3,0,2,1:T(1,128)S(1)} collective-permute-done((f32[1,3,16,3072]{3,0,2,1:T(1,128)}, f32[1,3,16,3072]{3,0,2,1:T(1,128)S(1)}, u32[]{:S(2)}, u32[]{:S(2)}) %collective-permute-start.2) | collective-permute-done | bytes 589856 | tf_op jit(solution)/shard_map/ppermute | solution.py:16
  80.1 0.1 maximum_bitcast_fusion
  80.3 0.3 copy.40
  80.6 1.6 gather_fusion.2
  82.2 5.4 %convolution_bitcast_fusion.3 = f32[48,2,8,128]{3,2,1,0:T(8,128)S(1)} fusion(f32[48,2,16,128]{3,2,1,0:T(8,128)} %bitcast.156, f32[48,2,128,128]{3,2,1,0:T(8,128)} %param.16), kind=kOutput, calls=%fused_computation.30 | convolution fusion | flops 301989888 | bytes 7471104 | tf_op jit(solution)/shard_map/nrfb,nrbc->fnc/dot_general | solution.py:93
  87.7 0.7 copy-done.8
  88.4 0.2 copy_bitcast_fusion
  88.7 0.6 gather_fusion.3
  89.3 0.1 copy_bitcast_fusion.1
  89.3 0.1 fusion.35
  89.4 0.4 copy-done.5
  89.8 7.2 %collective-permute-start.5 = (f32[64,1536]{1,0:T(8,128)S(1)}, f32[64,1536]{1,0:T(8,128)S(1)}, u32[]{:S(2)}, u32[]{:S(2)}) collective-permute-start(f32[64,1536]{1,0:T(8,128)S(1)} %get-tuple-element.12), channel_id=1, source_target_pairs={{1,0},{2,1},{3,2},{4,3},{5,4},{6,5},{7,6},{8,7},{9,8},{10,9},{11,1... | collective-permute-start | bytes 1179656 | tf_op jit(solution)/shard_map/ppermute | solution.py:17
  97.0 7.9 %collective-permute-done.4 = f32[64,1536]{1,0:T(8,128)S(1)} collective-permute-done((f32[64,1536]{1,0:T(8,128)S(1)}, f32[64,1536]{1,0:T(8,128)S(1)}, u32[]{:S(2)}, u32[]{:S(2)}) %collective-permute-start.4) | collective-permute-done | bytes 393248 | tf_op jit(solution)/shard_map/ppermute | solution.py:16
  104.9 0.3 pad_maximum_fusion.1
  105.2 3.0 %gather_fusion.4 = f32[144,64,128]{2,1,0:T(8,128)} fusion(f32[64,72,128]{2,0,1:T(8,128)S(1)} %pad_maximum_fusion.1, s32[1024]{0:T(1024)S(1)} %pad_clamp_fusion.1), kind=kCustom, calls=%fused_computation.4 | custom fusion | bytes 9437760 | tf_op jit(solution)/shard_map/gather | solution.py:39
  108.2 9.9 %fusion.12 = f32[48,8,8,128]{3,2,1,0:T(8,128)S(1)} fusion(f32[64,48,3,128]{3,0,2,1:T(8,128)} %bitcast.147, f32[1,48,3,128,128]{4,3,2,1,0:T(8,128)} %param.12), kind=kOutput, calls=%fused_computation.28 | convolution fusion | flops 1811939328 | bytes 15728640 | tf_op jit(solution)/shard_map/lnkb,nkbc->lnc/dot_general | solution.py:40
  118.1 1.7 convolution_bitcast_fusion
  119.9 0.3 fusion.4
  120.2 11.0 %all-gather.1 = f32[64,3072]{1,0:T(8,128)S(1)} all-gather(f32[16,3072]{1,0:T(8,128)S(1)} %fusion.4), channel_id=3, replica_groups=mesh['sec'=4,'dom'=64] {'sec'}, dimensions={0}, use_global_device_ids=true | all-gather | bytes 983040 | tf_op jit(solution)/shard_map/all_gather | solution.py:85
  131.2 0.1 slice_bitcast_fusion
  131.3 0.6 copy.49
  131.9 19.3 %collective-permute-start.7 = (f32[1,3,16,3072]{3,0,2,1:T(1,128)S(1)}, f32[1,3,16,3072]{3,0,2,1:T(1,128)S(1)}, u32[]{:S(2)}, u32[]{:S(2)}) collective-permute-start(f32[1,3,16,3072]{3,0,2,1:T(1,128)S(1)} %copy.49), channel_id=1, source_target_pairs={{1,0},{2,1},{3,2},{4,3},{5,4},{6,5},{7,6},{8,7},{9,8},{10,9},{11,1... | collective-permute-start | bytes 1769480 | tf_op jit(solution)/shard_map/ppermute | solution.py:17
  151.2 0.1 copy.70
  151.3 12.5 %collective-permute-done.7 = f32[1,3,16,3072]{3,0,2,1:T(1,128)S(1)} collective-permute-done((f32[1,3,16,3072]{3,0,2,1:T(1,128)S(1)}, f32[1,3,16,3072]{3,0,2,1:T(1,128)S(1)}, u32[]{:S(2)}, u32[]{:S(2)}) %collective-permute-start.7) | collective-permute-done | bytes 589856 | tf_op jit(solution)/shard_map/ppermute | solution.py:17
  163.7 7.6 %collective-permute-done.6 = f32[1,3,16,3072]{3,0,2,1:T(1,128)S(1)} collective-permute-done((f32[1,3,16,3072]{3,0,2,1:T(1,128)S(1)}, f32[1,3,16,3072]{3,0,2,1:T(1,128)S(1)}, u32[]{:S(2)}, u32[]{:S(2)}) %collective-permute-start.6) | collective-permute-done | bytes 589856 | tf_op jit(solution)/shard_map/ppermute | solution.py:16
  171.3 0.1 maximum_bitcast_fusion.1
  171.5 0.3 copy.52
  171.8 1.6 gather_fusion.5
  173.3 5.4 %convolution_bitcast_fusion.2 = f32[48,2,8,128]{3,2,1,0:T(8,128)S(1)} fusion(f32[48,2,16,128]{3,2,1,0:T(8,128)} %bitcast.155, f32[48,2,128,128]{3,2,1,0:T(8,128)} %param.16), kind=kOutput, calls=%fused_computation.29 | convolution fusion | flops 301989888 | bytes 7471104 | tf_op jit(solution)/shard_map/nrfb,nrbc->fnc/dot_general | solution.py:93
  178.8 1.3 select_bitcast_fusion
  (38 shorter events, 0.3 us)
Async XLA Ops:
  0.0 38.0 %copy-start = (f32[1,64,64]{2,1,0:T(8,128)S(1)}, f32[1,64,64]{2,1,0:T(8,128)}, u32[]{:S(2)}) copy-start(f32[1,64,64]{2,1,0:T(8,128)} %param.13) | copy-start | bytes 49156
  3.0 1.1 copy-start.3
  3.6 10.1 %copy-start.12 = (s32[1,48,3]{1,0,2:T(1,128)S(1)}, s32[1,48,3]{1,0,2:T(1,128)}, u32[]{:S(2)}) copy-start(s32[1,48,3]{1,0,2:T(1,128)} %param.11) | copy-start | bytes 1732
  4.1 18.4 %collective-permute-start = (f32[64,1536]{1,0:T(8,128)S(1)}, f32[64,1536]{1,0:T(8,128)S(1)}, u32[]{:S(2)}, u32[]{:S(2)}) collective-permute-start(f32[64,1536]{1,0:T(8,128)S(1)} %get-tuple-element.15), channel_id=1, source_target_pairs={{0,1},{1,2},{2,3},{3,4},{4,5},{5,6},{6,7},{7,8},{8,9},{9,10},{10,1... | collective-permute-start | bytes 1179656 | tf_op jit(solution)/shard_map/ppermute | solution.py:16
  5.8 16.8 %collective-permute-start.1 = (f32[64,1536]{1,0:T(8,128)S(1)}, f32[64,1536]{1,0:T(8,128)S(1)}, u32[]{:S(2)}, u32[]{:S(2)}) collective-permute-start(f32[64,1536]{1,0:T(8,128)S(1)} %get-tuple-element.16), channel_id=1, source_target_pairs={{1,0},{2,1},{3,2},{4,3},{5,4},{6,5},{7,6},{8,7},{9,8},{10,9},{11,1... | collective-permute-start | bytes 1179656 | tf_op jit(solution)/shard_map/ppermute | solution.py:17
  13.9 8.7 %copy-start.4 = (f32[64,48,128]{2,0,1:T(8,128)S(1)}, f32[64,48,128]{2,0,1:T(8,128)}, u32[]{:S(2)}) copy-start(f32[64,48,128]{2,0,1:T(8,128)} %copy-done.3) | copy-start | bytes 4718596
  36.6 1.9 %copy-start.7 = (f32[1,64,6144]{2,1,0:T(8,128)S(1)}, f32[1,64,6144]{2,1,0:T(8,128)}, u32[]{:S(2)}) copy-start(f32[1,64,6144]{2,1,0:T(8,128)} %param.9) | copy-start | bytes 4718596
  38.5 3.1 %copy-start.10 = (f32[1,16,16]{2,1,0:T(8,128)S(1)}, f32[1,16,16]{2,1,0:T(8,128)}, u32[]{:S(2)}) copy-start(f32[1,16,16]{2,1,0:T(8,128)} %param.14) | copy-start | bytes 3076
  41.6 46.1 %copy-start.1 = (f32[64,6144]{1,0:T(8,128)}, f32[64,6144]{1,0:T(8,128)S(1)}, u32[]{:S(2)}) copy-start(f32[64,6144]{1,0:T(8,128)S(1)} %convolution_bitcast_fusion.1) | copy-start | bytes 4718596
  41.9 17.8 %copy-start.11 = (s32[6144]{0:T(1024)S(1)}, s32[6144]{0:T(1024)}, u32[]{:S(2)}) copy-start(s32[6144]{0:T(1024)} %param.17) | copy-start | bytes 73732
  42.0 17.8 %copy-start.13 = (s32[48,2]{0,1:T(2,128)S(1)}, s32[48,2]{0,1:T(2,128)}, u32[]{:S(2)}) copy-start(s32[48,2]{0,1:T(2,128)} %param.15) | copy-start | bytes 1156
  53.2 19.4 %collective-permute-start.3 = (f32[1,3,16,3072]{3,0,2,1:T(1,128)}, f32[1,3,16,3072]{3,0,2,1:T(1,128)S(1)}, u32[]{:S(2)}, u32[]{:S(2)}) collective-permute-start(f32[1,3,16,3072]{3,0,2,1:T(1,128)} %copy.37), channel_id=1, source_target_pairs={{1,0},{2,1},{3,2},{4,3},{5,4},{6,5},{7,6},{8,7},{9,8},{10,9},{11,1... | collective-permute-start | bytes 1769480 | tf_op jit(solution)/shard_map/ppermute | solution.py:17
  59.7 20.4 %collective-permute-start.2 = (f32[1,3,16,3072]{3,0,2,1:T(1,128)}, f32[1,3,16,3072]{3,0,2,1:T(1,128)S(1)}, u32[]{:S(2)}, u32[]{:S(2)}) collective-permute-start(f32[1,3,16,3072]{3,0,2,1:T(1,128)} %copy.37), channel_id=1, source_target_pairs={{0,1},{1,2},{2,3},{3,4},{4,5},{5,6},{6,7},{7,8},{8,9},{9,10},{10,1... | collective-permute-start | bytes 1769480 | tf_op jit(solution)/shard_map/ppermute | solution.py:16
  87.7 0.8 copy-start.8
  88.7 1.1 copy-start.5
  89.8 15.1 %copy-start.6 = (f32[64,48,128]{2,0,1:T(8,128)S(1)}, f32[64,48,128]{2,0,1:T(8,128)}, u32[]{:S(2)}) copy-start(f32[64,48,128]{2,0,1:T(8,128)} %copy-done.5) | copy-start | bytes 4718596
  89.8 15.0 %collective-permute-start.4 = (f32[64,1536]{1,0:T(8,128)S(1)}, f32[64,1536]{1,0:T(8,128)S(1)}, u32[]{:S(2)}, u32[]{:S(2)}) collective-permute-start(f32[64,1536]{1,0:T(8,128)S(1)} %get-tuple-element.11), channel_id=1, source_target_pairs={{0,1},{1,2},{2,3},{3,4},{4,5},{5,6},{6,7},{7,8},{8,9},{9,10},{10,1... | collective-permute-start | bytes 1179656 | tf_op jit(solution)/shard_map/ppermute | solution.py:16
  89.8 15.1 %collective-permute-start.5 = (f32[64,1536]{1,0:T(8,128)S(1)}, f32[64,1536]{1,0:T(8,128)S(1)}, u32[]{:S(2)}, u32[]{:S(2)}) collective-permute-start(f32[64,1536]{1,0:T(8,128)S(1)} %get-tuple-element.12), channel_id=1, source_target_pairs={{1,0},{2,1},{3,2},{4,3},{5,4},{6,5},{7,6},{8,7},{9,8},{10,9},{11,1... | collective-permute-start | bytes 1179656 | tf_op jit(solution)/shard_map/ppermute | solution.py:17
  108.2 9.9 %copy-start.2 = (f32[64,6144]{1,0:T(8,128)S(1)}, f32[64,6144]{1,0:T(8,128)}, u32[]{:S(2)}) copy-start(f32[64,6144]{1,0:T(8,128)} %copy-done.1) | copy-start | bytes 4718596
  108.2 9.9 %copy-start.9 = (f32[48,2,8,128]{3,2,0,1:T(8,128)S(1)}, f32[48,2,8,128]{3,2,0,1:T(8,128)}, u32[]{:S(2)}) copy-start(f32[48,2,8,128]{3,2,0,1:T(8,128)} %copy-done.8) | copy-start | bytes 1179652
  131.9 31.8 %collective-permute-start.7 = (f32[1,3,16,3072]{3,0,2,1:T(1,128)S(1)}, f32[1,3,16,3072]{3,0,2,1:T(1,128)S(1)}, u32[]{:S(2)}, u32[]{:S(2)}) collective-permute-start(f32[1,3,16,3072]{3,0,2,1:T(1,128)S(1)} %copy.49), channel_id=1, source_target_pairs={{1,0},{2,1},{3,2},{4,3},{5,4},{6,5},{7,6},{8,7},{9,8},{10,9},{11,1... | collective-permute-start | bytes 1769480 | tf_op jit(solution)/shard_map/ppermute | solution.py:17
  151.2 20.2 %collective-permute-start.6 = (f32[1,3,16,3072]{3,0,2,1:T(1,128)S(1)}, f32[1,3,16,3072]{3,0,2,1:T(1,128)S(1)}, u32[]{:S(2)}, u32[]{:S(2)}) collective-permute-start(f32[1,3,16,3072]{3,0,2,1:T(1,128)S(1)} %copy.49), channel_id=1, source_target_pairs={{0,1},{1,2},{2,3},{3,4},{4,5},{5,6},{6,7},{7,8},{8,9},{9,10},{10,1... | collective-permute-start | bytes 1769480 | tf_op jit(solution)/shard_map/ppermute | solution.py:16
where the time goes:
time: 182 us; the launch traced here: 180 us
  waiting for transfers between devices  56.5 us (31%)
  starting transfers between devices  42.6 us (23%)
  matrix products  35.9 us (20%)
  local copies, waits for them, and re-layouts  21.6 us (12%)
  blocking collectives  20.7 us (11%)
  other arithmetic  2.41 us (1%)
    ppermute x4, starting transfers between devices, extended_2(): after = lax.ppermute(initial, axis, down)  40.9 us
    ppermute x4, waiting for transfers between devices, extended_2(): before = lax.ppermute(last, axis, up)  31.5 us
    ppermute x4, waiting for transfers between devices, extended_2(): after = lax.ppermute(initial, axis, down)  25 us
    all_gather x2, blocking collectives, local(): sections = lax.all_gather(surface_flux[None], 'sec', axis=0, tiled=True)  20.7 us
    dot_general x2, matrix products, apply_operator(): jnp.einsum('lnkb,nkbc->lnc', picked, weights, precision=lax.Precision.HIG...  19.6 us
    dot_general x2, matrix products, local(): jnp.einsum('nrfb,nrbc->fnc', chosen, remap_weight, precision=lax.Precisio...  10.9 us
    gather x2, local copies, waits for them, and re-layouts, apply_operator(): everything[:, pattern, :].reshape(levels, block_count, -1, block_size)  6.01 us
    dot_general x2, matrix products, local(): jnp.dot(vertical_matrix, updated, precision=lax.Precision.HIGHEST)  4.76 us
  transfers between devices with their start and end apart: 8, of which 6 were waited for; matrix products, arithmetic and copies ran while one was open for 0% of the time, Pallas kernels for 0%

commit v1 on v0

v1 whole, which is shorter than its diff:
```python
import functools

import jax
import jax.numpy as jnp
from jax import lax
from jax.experimental import pallas as pl
from jax.experimental.pallas import tpu as pltpu
from jax.sharding import PartitionSpec as P

MESH = pl.DeviceIdType.MESH
STEPS = 2
WCH = 4


def split(v):
    hi = v.astype(jnp.bfloat16)
    lo = (v - hi.astype(jnp.float32)).astype(jnp.bfloat16)
    return hi, lo


def mm(a, b):
    return jnp.dot(a, b, preferred_element_type=jnp.float32)


def kernel(
    secs,
    doms,
    state,
    send_list,
    op_index,
    op_weight,
    vertical,
    flux_weight,
    remap_index,
    remap_weight,
    wet,
    out,
    x,
    eb,
    wf,
    wb,
    rf,
    rb,
    ys,
    sendbuf,
    land,
    fbuf,
    cand0,
    cand1,
    in_sem,
    w_sem,
    r_sem,
    out_sem,
    hs_sem,
    hr_sem,
    fs_sem,
    fr_sem,
    gs_sem,
    gr_sem,
):
    nb, levels, bs = x.shape[1:]
    nh = land.shape[2]
    kd = wb.shape[1]
    nba = nb // 2
    nf = fbuf.shape[2]
    sur = nf // 2
    natm = secs - 1

    sec = lax.axis_index("sec")
    dom = lax.axis_index("dom")
    nxt = lax.rem(dom + 1, doms)
    prv = lax.rem(dom + doms - 1, doms)
    ocean = natm
    is_ocean = sec == ocean
    cands = (cand0, cand1)

    def state_copy(n):
        cols = pl.ds(pl.multiple_of(n * bs, bs), bs)
        return pltpu.make_async_copy(state.at[0, :, cols], x.at[0, n], in_sem)

    @pl.loop(0, nb)
    def _(n):
        state_copy(n).start()

    wn = nb // WCH
    w_copies = [
        pltpu.make_async_copy(
            op_weight.at[pl.ds(c * wn, wn)], wf.at[pl.ds(c * wn, wn)], w_sem.at[c]
        )
        for c in range(WCH)
    ]
    for c in w_copies:
        c.start()
    r_copy = pltpu.make_async_copy(remap_weight, rf, r_sem)

    @pl.when(is_ocean)
    def _():
        r_copy.start()

    barrier = pltpu.get_barrier_semaphore()

    def greet(s, d):
        pl.semaphore_signal(barrier, inc=1, device_id={"sec": s, "dom": d}, device_id_type=MESH)

    greet(sec, prv)
    greet(sec, nxt)

    @pl.when(is_ocean)
    def _():
        for s in range(natm):
            greet(s, dom)
        pl.semaphore_wait(barrier, 2 + natm)

    @pl.when(jnp.logical_not(is_ocean))
    def _():
        greet(ocean, dom)
        pl.semaphore_wait(barrier, 3)

    def halo(step, to_next):
        src = 1 if to_next else 0
        return pltpu.make_async_remote_copy(
            src_ref=sendbuf.at[step, src],
            dst_ref=land.at[step, 1 - src],
            send_sem=hs_sem.at[step, src],
            recv_sem=hr_sem.at[step, 1 - src],
            device_id={"sec": sec, "dom": nxt if to_next else prv},
            device_id_type=MESH,
        )

    def flux(step, s):
        return pltpu.make_async_remote_copy(
            src_ref=fbuf.at[step],
            dst_ref=cands[step].at[1, s],
            send_sem=fs_sem.at[step],
            recv_sem=fr_sem.at[step, s],
            device_id={"sec": ocean, "dom": dom},
            device_id_type=MESH,
        )

    def forward(step, s, to_next):
        o = 0 if to_next else 2
        return pltpu.make_async_remote_copy(
            src_ref=cands[step].at[1, s],
            dst_ref=cands[step].at[o, s],
            send_sem=gs_sem.at[step, s, o // 2],
            recv_sem=gr_sem.at[step, s, o // 2],
            device_id={"sec": ocean, "dom": nxt if to_next else prv},
            device_id_type=MESH,
        )

    def send_halo(step, cur):
        for to_next in (True, False):
            j = 1 if to_next else 0

            @pl.loop(0, nh)
            def _(h):
                sendbuf[step, j, h] = x[cur, send_list[0, 0, j, h]]

            halo(step, to_next).start()

    def split_own(cur):
        @pl.loop(0, nb // 4)
        def _(i):
            for u in range(4):
                hi, lo = split(x[cur, i * 4 + u])
                eb[i * 4 + u, :levels] = hi
                eb[i * 4 + u, levels:] = lo

    pltpu.make_async_copy(x.at[0], x.at[0], in_sem).wait()

    send_halo(0, 0)
    split_own(0)

    vh, vl = split(vertical[0])
    v3 = jnp.concatenate([vh, vh, vl], axis=1)
    fh, fl = split(flux_weight[0])
    f3 = jnp.concatenate([fh, fh, fl], axis=1)

    for c in range(WCH):
        w_copies[c].wait()

        @pl.loop(c * wn, (c + 1) * wn)
        def _(n):
            hi, lo = split(wf[n])
            wb[n, :, :bs] = hi
            wb[n, :, bs:] = lo

    @pl.when(is_ocean)
    def _():
        r_copy.wait()

        @pl.loop(0, nb)
        def _(n):
            hi, lo = split(rf[n])
            rb[n, :, :bs] = hi
            rb[n, :, bs:] = lo

    def out_copy(buf, n):
        cols = pl.ds(pl.multiple_of(n * bs, bs), bs)
        return pltpu.make_async_copy(x.at[buf, n], out.at[0, :, cols], out_sem)

    for step in range(STEPS):
        cur, new = step, step + 1
        halo(step, True).wait_recv()
        halo(step, False).wait_recv()
        for half in range(2):

            @pl.loop(0, nh // 4)
            def _(i):
                for u in range(4):
                    h = i * 4 + u
                    hi, lo = split(land[step, half, h])
                    eb[nb + half * nh + h, :levels] = hi
                    eb[nb + half * nh + h, levels:] = lo

        @pl.loop(0, nb // 4)
        def _(i):
            for u in range(2):
                parts = []
                for t in range(2):
                    n = i * 4 + u * 2 + t
                    lhs = jnp.concatenate(
                        [eb[op_index[k, 0, n]] for k in range(op_index.shape[0])], axis=1
                    )
                    r = mm(lhs, wb[n])
                    y = x[cur, n] + (r[:levels, :bs] + (r[:levels, bs:] + r[levels:, :bs]))
                    parts.append(split(y))
                hi = jnp.concatenate([parts[0][0], parts[1][0]], axis=1)
                lo = jnp.concatenate([parts[0][1], parts[1][1]], axis=1)
                m = i * 2 + u
                ys[m, :levels] = hi
                ys[m, levels : 2 * levels] = lo
                ys[m, 2 * levels :] = hi

        @pl.loop(0, nb // 8)
        def _(i):
            for u in range(4):
                m = i * 4 + u
                r = mm(v3, ys[m])
                x[new, 2 * m] = r[:, :bs]
                x[new, 2 * m + 1] = r[:, bs:]

        @pl.when(jnp.logical_not(is_ocean))
        def _():
            @pl.loop(0, nba // 4)
            def _(i):
                for u in range(2):
                    b = i * 4 + u * 2
                    p = jnp.concatenate(
                        [
                            jnp.concatenate([x[new, b, levels - sur :], x[new, b + 1, levels - sur :]], axis=1),
                            jnp.concatenate(
                                [x[new, nba + b, levels - sur :], x[new, nba + b + 1, levels - sur :]], axis=1
                            ),
                        ],
                        axis=0,
                    )
                    hi, lo = split(p)
                    f = jnp.tanh(mm(f3, jnp.concatenate([hi, lo, hi], axis=0)))
                    fbuf[step, b] = f[:, :bs]
                    fbuf[step, b + 1] = f[:, bs:]

            flux(step, sec).start()
            if step + 1 < STEPS:
                send_halo(step + 1, new)
            else:

                @pl.loop(0, nb)
                def _(n):
                    out_copy(new, n).start()

        @pl.when(is_ocean)
        def _():
            for s in reversed(range(natm)):
                flux(step, s).wait_recv()
                forward(step, s, True).start()
                forward(step, s, False).start()
            for s in reversed(range(natm)):
                forward(step, s, True).wait_recv()
                forward(step, s, False).wait_recv()
            cflat = cands[step].reshape(3 * natm * nba, nf, bs)

            @pl.loop(0, nb // 2)
            def _(i):
                for u in range(2):
                    n = i * 2 + u
                    c = jnp.concatenate(
                        [cflat[remap_index[j, n]] for j in range(remap_index.shape[0])], axis=1
                    )
                    hi, lo = split(c)
                    r = mm(jnp.concatenate([hi, lo], axis=0), rb[n])
                    g = r[:nf, :bs] + (r[:nf, bs:] + r[nf:, :bs])
                    mask = wet[pl.ds(n, 1), :].astype(jnp.float32)
                    x[new, n, :nf] = mask * (x[new, n, :nf] + g)
                    x[new, n, nf:] = mask * x[new, n, nf:]

            if step + 1 < STEPS:
                send_halo(step + 1, new)
            else:

                @pl.loop(0, nb)
                def _(n):
                    out_copy(new, n).start()

        if step + 1 < STEPS:
            split_own(new)

    for step in range(STEPS):
        halo(step, True).wait_send()
        halo(step, False).wait_send()

        @pl.when(is_ocean)
        def _():
            for s in range(natm):
                forward(step, s, True).wait_send()
                forward(step, s, False).wait_send()

        @pl.when(jnp.logical_not(is_ocean))
        def _():
            flux(step, sec).wait_send()

    pltpu.make_async_copy(x.at[STEPS], x.at[STEPS], out_sem).wait()


def solution(mesh):
    secs, doms = mesh.shape["sec"], mesh.shape["dom"]

    def local(
        state, send_list, op_index, op_weight, vertical, flux_weight, remap_index, remap_weight, wet_mask
    ):
        levels, slots = state.shape[1:]
        nk, bs = op_weight.shape[2:4]
        nb = slots // bs
        nh = send_list.shape[3]
        nr = remap_weight.shape[1]
        nf = flux_weight.shape[1]
        natm = secs - 1
        nba = nb // 2
        f32, bf16 = jnp.float32, jnp.bfloat16
        hbm = pl.BlockSpec(memory_space=pl.ANY)
        smem = pl.BlockSpec(memory_space=pltpu.SMEM)
        vmem = pl.BlockSpec(memory_space=pltpu.VMEM)
        dma = pltpu.SemaphoreType.DMA
        return pl.pallas_call(
            functools.partial(kernel, secs, doms),
            out_shape=jax.ShapeDtypeStruct(state.shape, f32),
            in_specs=[hbm, smem, smem, hbm, vmem, vmem, smem, hbm, vmem],
            out_specs=hbm,
            scratch_shapes=[
                pltpu.VMEM((STEPS + 1, nb, levels, bs), f32),
                pltpu.VMEM((nb + 2 * nh, 2 * levels, bs), bf16),
                pltpu.VMEM((nb, nk * bs, bs), f32),
                pltpu.VMEM((nb, nk * bs, 2 * bs), bf16),
                pltpu.VMEM((nb, nr * bs, bs), f32),
                pltpu.VMEM((nb, nr * bs, 2 * bs), bf16),
                pltpu.VMEM((nb // 2, 3 * levels, 2 * bs), bf16),
                pltpu.VMEM((STEPS, 2, nh, levels, bs), f32),
                pltpu.VMEM((STEPS, 2, nh, levels, bs), f32),
                pltpu.VMEM((STEPS, nba, nf, bs), f32),
                pltpu.VMEM((3, natm, nba, nf, bs), f32),
                pltpu.VMEM((3, natm, nba, nf, bs), f32),
                dma,
                dma((WCH,)),
                dma,
                dma,
                dma((STEPS, 2)),
                dma((STEPS, 2)),
                dma((STEPS,)),
                dma((STEPS, natm)),
                dma((STEPS, natm, 2)),
                dma((STEPS, natm, 2)),
            ],
            compiler_params=pltpu.CompilerParams(
                collective_id=0, has_side_effects=True, vmem_limit_bytes=66 * 1000 * 1000
            ),
        )(
            state,
            send_list,
            op_index.transpose(2, 0, 1),
            op_weight.reshape(nb, nk * bs, bs),
            vertical,
            flux_weight,
            remap_index.T,
            remap_weight.reshape(nb, nr * bs, bs),
            wet_mask.reshape(nb, bs),
        )

    in_specs = (
        P("sec", None, "dom"),
        P("sec", "dom", None, None),
        P("sec", "dom", None),
        P("sec", "dom", None, None, None),
        P("sec", None, None),
        P("sec", None, None),
        P("dom", None),
        P("dom", None, None, None),
        P("dom"),
    )
    return jax.shard_map(
        local, mesh=mesh, in_specs=in_specs, out_specs=P("sec", None, "dom"), check_vma=False
    )
```

time: 182 us -> 85.7 us (0.47)
  Pallas kernels: 0 us -> 82.9 us
  waiting for transfers between devices: 56.5 us -> 0 us
  starting transfers between devices: 42.6 us -> 0 us
  matrix products: 35.9 us -> 0 us
  blocking collectives: 20.7 us -> 0 us
  local copies, waits for them, and re-layouts: 21.6 us -> 2.66 us
  other arithmetic: 2.41 us -> 0 us
    pallas_call x0 -> x1, Pallas kernels: none -> 82.9 us  [local(): pl.pallas_call(functools.partial(kernel, secs, doms), out_shape=jax.Shape...]
    ppermute x8 -> x0, waiting for transfers between devices: 56.5 us -> none  [the longest x4 31.5 us: extended_2(): before = lax.ppermute(last, axis, up)]
    ppermute x8 -> x0, starting transfers between devices: 42.6 us -> none  [the longest x4 40.9 us: extended_2(): after = lax.ppermute(initial, axis, down)]
    dot_general x8 -> x0, matrix products: 35.9 us -> none  [the longest x2 19.6 us: apply_operator(): jnp.einsum('lnkb,nkbc->lnc', picked, weights, precision=lax.Precision.HIG...]
    all_gather x2 -> x0, blocking collectives: 20.7 us -> none  [local(): sections = lax.all_gather(surface_flux[None], 'sec', axis=0, tiled=True)]
    gather x6 -> x0, local copies, waits for them, and re-layouts: 10.4 us -> none  [the longest x2 6.01 us: apply_operator(): everything[:, pattern, :].reshape(levels, block_count, -1, block_size)]
    broadcast_in_dim x2 -> x0, local copies, waits for them, and re-layouts: 2.03 us -> none  [local(): nearby = extended_2(atmosphere[None], (('dom', 0),), 1)]
    unnamed x35 -> x1, local copies, waits for them, and re-layouts: 4.39 us -> 2.66 us
  transfers between devices with their start and end apart: 8 -> 0, of which waited for: 6 -> 0; matrix products, arithmetic and copies ran while one was open for 0% -> 0% of each run, Pallas kernels for 0% -> 0%
where the time goes in v1:
time: 85.7 us; the launch traced here: 85.5 us
  Pallas kernels  82.9 us (97%)
  local copies, waits for them, and re-layouts  2.66 us (3%)
    pallas_call x1, Pallas kernels, local(): pl.pallas_call(functools.partial(kernel, secs, doms), out_shape=jax.Shape...  82.9 us
    unnamed x1, local copies, waits for them, and re-layouts  2.66 us

profile of v1, /device:TPU:3, one launch (start us, length us, event | category | flops | bytes accessed | tf_op | source)
XLA Modules:
  0.0 85.5 jit_solution(15811906337139474819)
XLA Ops:
  0.0 82.9 %shard_map.91 = f32[1,64,6144]{2,1,0:T(8,128)} custom-call(f32[1,64,6144]{2,1,0:T(8,128)} %state.1, s32[1,1,2,12]{3,2,1,0:T(2,128)} %send_list.1, s32[3,1,48]{2,1,0:T(1,128)} %bitcast.8, f32[48,384,128]{2,1,0:T(8,128)} %bitcast.5, f32[1,64,64]{2,1,0:T(8,128)} %vertical.1, f32[1,16,16]{2,1,0:T(8,128)} %flux_weight.1, s32[2,48]{1,0:T(2,128)} %bitcast.9, ...), custom_call_target="tpu_custom_call" | custom-call | tf_op jit(solution)/shard_map/pallas_call | solution.py:344
  82.9 2.7 %copy.11 = f32[1,64,6144]{2,1,0:T(8,128)} copy(f32[1,64,6144]{2,1,0:T(8,128)} %shard_map.91) | data formatting | bytes 3145728

commit v2 on v1

v2 whole, which is shorter than its diff:
```python
import functools

import jax
import jax.numpy as jnp
from jax import lax
from jax.experimental import pallas as pl
from jax.experimental.pallas import tpu as pltpu
from jax.sharding import PartitionSpec as P

MESH = pl.DeviceIdType.MESH
STEPS = 2
WCH = 4
FCH = 2


def split(v):
    hi = v.astype(jnp.bfloat16)
    lo = (v - hi.astype(jnp.float32)).astype(jnp.bfloat16)
    return hi, lo


def mm(a, b):
    return jnp.dot(a, b, preferred_element_type=jnp.float32)


def kernel(
    secs,
    doms,
    state,
    send_list,
    op_index,
    op_weight,
    vertical,
    flux_weight,
    remap_index,
    remap_weight,
    wet,
    out,
    x,
    eb,
    wf,
    wb,
    rf,
    rb,
    ys,
    sendbuf,
    land,
    fbuf,
    relay,
    cand0,
    cand1,
    in_sem,
    w_sem,
    r_sem,
    out_sem,
    hs_sem,
    hr_sem,
    fs_sem,
    fr_sem,
    gs_sem,
    gr_sem,
):
    nb, levels, bs = x.shape[1:]
    nh = land.shape[2]
    kd = wb.shape[1]
    nba = nb // 2
    nf = fbuf.shape[2]
    sur = nf // 2
    natm = secs - 1

    sec = lax.axis_index("sec")
    dom = lax.axis_index("dom")
    nxt = lax.rem(dom + 1, doms)
    prv = lax.rem(dom + doms - 1, doms)
    ocean = natm
    hub = natm - 1
    is_ocean = sec == ocean
    is_hub = sec == hub
    fc = nba // FCH
    around = ((0, nxt), (2, prv), (1, dom))
    rows = (pl.ds(nf, levels - nf), pl.ds(0, nf))
    cands = (cand0, cand1)

    def state_copy(n):
        cols = pl.ds(pl.multiple_of(n * bs, bs), bs)
        return pltpu.make_async_copy(state.at[0, :, cols], x.at[0, n], in_sem)

    @pl.loop(0, nb)
    def _(n):
        state_copy(n).start()

    wn = nb // WCH
    w_copies = [
        pltpu.make_async_copy(
            op_weight.at[pl.ds(c * wn, wn)], wf.at[pl.ds(c * wn, wn)], w_sem.at[c]
        )
        for c in range(WCH)
    ]
    for c in w_copies:
        c.start()
    r_copy = pltpu.make_async_copy(remap_weight, rf, r_sem)

    @pl.when(is_ocean)
    def _():
        r_copy.start()

    barrier = pltpu.get_barrier_semaphore()

    def greet(s, d):
        pl.semaphore_signal(barrier, inc=1, device_id={"sec": s, "dom": d}, device_id_type=MESH)

    greet(sec, prv)
    greet(sec, nxt)

    @pl.when(is_ocean)
    def _():
        for _, d in around:
            greet(hub, d)
        pl.semaphore_wait(barrier, 5)

    @pl.when(is_hub)
    def _():
        for _, d in around:
            greet(ocean, d)
        for s in range(hub):
            greet(s, dom)
        pl.semaphore_wait(barrier, 5 + hub)

    @pl.when(sec < hub)
    def _():
        greet(hub, dom)
        pl.semaphore_wait(barrier, 3)

    def halo(step, to_next, part):
        src = 1 if to_next else 0
        return pltpu.make_async_remote_copy(
            src_ref=sendbuf.at[step, src, :, rows[part]],
            dst_ref=land.at[step, 1 - src, :, rows[part]],
            send_sem=hs_sem.at[step, src, part],
            recv_sem=hr_sem.at[step, 1 - src, part],
            device_id={"sec": sec, "dom": nxt if to_next else prv},
            device_id_type=MESH,
        )

    def flux(step, s, c):
        return pltpu.make_async_remote_copy(
            src_ref=fbuf.at[step, pl.ds(c * fc, fc)],
            dst_ref=relay.at[step, s, pl.ds(c * fc, fc)],
            send_sem=fs_sem.at[step, c],
            recv_sem=fr_sem.at[step, s, c],
            device_id={"sec": hub, "dom": dom},
            device_id_type=MESH,
        )

    def forward(step, s, c, o, d):
        src = fbuf.at[step] if s == hub else relay.at[step, s]
        return pltpu.make_async_remote_copy(
            src_ref=src.at[pl.ds(c * fc, fc)],
            dst_ref=cands[step].at[o, s, pl.ds(c * fc, fc)],
            send_sem=gs_sem.at[step, s, c, o],
            recv_sem=gr_sem.at[step, s, c, o],
            device_id={"sec": ocean, "dom": d},
            device_id_type=MESH,
        )

    def send_halo(step, cur, part):
        for to_next in (True, False):
            j = 1 if to_next else 0

            @pl.loop(0, nh)
            def _(h):
                sendbuf[step, j, h, rows[part]] = x[cur, send_list[0, 0, j, h], rows[part]]

            halo(step, to_next, part).start()

    def put_split(n, v, part):
        start, size = rows[part].start, rows[part].size
        hi, lo = split(v)
        eb[n, pl.ds(start, size)] = hi
        eb[n, pl.ds(levels + start, size)] = lo

    def split_own(cur, part):
        @pl.loop(0, nb // 4)
        def _(i):
            for u in range(4):
                put_split(i * 4 + u, x[cur, i * 4 + u, rows[part]], part)

    def take_halo(step, part):
        halo(step, True, part).wait_recv()
        halo(step, False, part).wait_recv()
        for half in range(2):

            @pl.loop(0, nh // 4)
            def _(i):
                for u in range(4):
                    h = i * 4 + u
                    put_split(nb + half * nh + h, land[step, half, h, rows[part]], part)

    pltpu.make_async_copy(x.at[0], x.at[0], in_sem).wait()

    for part in range(2):
        send_halo(0, 0, part)
    for part in range(2):
        split_own(0, part)

    vh, vl = split(vertical[0])
    v3 = jnp.concatenate([vh, vh, vl], axis=1)
    fh, fl = split(flux_weight[0])
    f3 = jnp.concatenate([fh, fh, fl], axis=1)

    for c in range(WCH):
        w_copies[c].wait()

        @pl.loop(c * wn, (c + 1) * wn)
        def _(n):
            hi, lo = split(wf[n])
            wb[n, :, :bs] = hi
            wb[n, :, bs:] = lo

    @pl.when(is_ocean)
    def _():
        r_copy.wait()

        @pl.loop(0, nb)
        def _(n):
            hi, lo = split(rf[n])
            rb[n, :, :bs] = hi
            rb[n, :, bs:] = lo

    def send_out(part):
        @pl.loop(0, nb)
        def _(n):
            cols = pl.ds(pl.multiple_of(n * bs, bs), bs)
            pltpu.make_async_copy(
                x.at[STEPS, n, rows[part]], out.at[0, rows[part], cols], out_sem
            ).start()

    def step_chunk(cur, new, c):
        hp = nba // 2
        cp = hp // FCH

        def pair(j):
            return j + c * cp + j // cp * (hp - cp)

        @pl.loop(0, cp)
        def _(i):
            for u in range(2):
                m = pair(i * 2 + u)
                parts = []
                for t in range(2):
                    n = m * 2 + t
                    lhs = jnp.concatenate(
                        [eb[op_index[k, 0, n]] for k in range(op_index.shape[0])], axis=1
                    )
                    r = mm(lhs, wb[n])
                    y = x[cur, n] + (r[:levels, :bs] + (r[:levels, bs:] + r[levels:, :bs]))
                    parts.append(split(y))
                hi = jnp.concatenate([parts[0][0], parts[1][0]], axis=1)
                lo = jnp.concatenate([parts[0][1], parts[1][1]], axis=1)
                ys[m, :levels] = hi
                ys[m, levels : 2 * levels] = lo
                ys[m, 2 * levels :] = hi

        @pl.loop(0, cp // 2)
        def _(i):
            for u in range(4):
                m = pair(i * 4 + u)
                r = mm(v3, ys[m])
                x[new, 2 * m] = r[:, :bs]
                x[new, 2 * m + 1] = r[:, bs:]

    for step in range(STEPS):
        cur, new = step, step + 1
        last = new == STEPS
        if step == 0:
            take_halo(step, 0)
            take_halo(step, 1)
        else:

            @pl.when(jnp.logical_not(is_ocean))
            def _():
                take_halo(step, 0)

            take_halo(step, 1)

        for c in range(FCH):
            step_chunk(cur, new, c)

            @pl.when(jnp.logical_not(is_ocean))
            def _():
                @pl.loop(0, fc // 4)
                def _(i):
                    for u in range(2):
                        b = c * fc + i * 4 + u * 2
                        p = jnp.concatenate(
                            [
                                jnp.concatenate([x[new, b, levels - sur :], x[new, b + 1, levels - sur :]], axis=1),
                                jnp.concatenate(
                                    [x[new, nba + b, levels - sur :], x[new, nba + b + 1, levels - sur :]], axis=1
                                ),
                            ],
                            axis=0,
                        )
                        hi, lo = split(p)
                        f = jnp.tanh(mm(f3, jnp.concatenate([hi, lo, hi], axis=0)))
                        fbuf[step, b] = f[:, :bs]
                        fbuf[step, b + 1] = f[:, bs:]

            @pl.when(sec < hub)
            def _():
                flux(step, sec, c).start()

            @pl.when(is_hub)
            def _():
                for o, d in around:
                    forward(step, hub, c, o, d).start()

        @pl.when(is_hub)
        def _():
            for c in range(FCH):
                for s in range(hub):
                    flux(step, s, c).wait_recv()
                    for o, d in around:
                        forward(step, s, c, o, d).start()

        @pl.when(jnp.logical_not(is_ocean))
        def _():
            for part in range(2):
                if last:
                    send_out(part)
                else:
                    send_halo(step + 1, new, part)
            if not last:
                for part in range(2):
                    split_own(new, part)

        @pl.when(is_ocean)
        def _():
            @pl.loop(0, nb // 4)
            def _(i):
                for u in range(4):
                    n = i * 4 + u
                    x[new, n, nf:] = wet[pl.ds(n, 1), :].astype(jnp.float32) * x[new, n, nf:]

            if last:
                send_out(0)
            else:
                send_halo(step + 1, new, 0)
                split_own(new, 0)
                take_halo(step + 1, 0)

            for c in range(FCH):
                for s in range(natm):
                    for o, d in around:
                        forward(step, s, c, o, d).wait_recv()
            cflat = cands[step].reshape(3 * natm * nba, nf, bs)

            @pl.loop(0, nb // 4)
            def _(i):
                for u in range(4):
                    n = i * 4 + u
                    c = jnp.concatenate(
                        [cflat[remap_index[j, n]] for j in range(remap_index.shape[0])], axis=1
                    )
                    hi, lo = split(c)
                    r = mm(jnp.concatenate([hi, lo], axis=0), rb[n])
                    g = r[:nf, :bs] + (r[:nf, bs:] + r[nf:, :bs])
                    mask = wet[pl.ds(n, 1), :].astype(jnp.float32)
                    x[new, n, :nf] = mask * (x[new, n, :nf] + g)

            if last:
                send_out(1)
            else:
                send_halo(step + 1, new, 1)
                split_own(new, 1)

    for step in range(STEPS):
        for part in range(2):
            halo(step, True, part).wait_send()
            halo(step, False, part).wait_send()

        for c in range(FCH):

            @pl.when(is_hub)
            def _():
                for s in range(natm):
                    for o, d in around:
                        forward(step, s, c, o, d).wait_send()

            @pl.when(sec < hub)
            def _():
                flux(step, sec, c).wait_send()

    pltpu.make_async_copy(x.at[STEPS], x.at[STEPS], out_sem).wait()


def solution(mesh):
    secs, doms = mesh.shape["sec"], mesh.shape["dom"]

    def local(
        state, send_list, op_index, op_weight, vertical, flux_weight, remap_index, remap_weight, wet_mask
    ):
        levels, slots = state.shape[1:]
        nk, bs = op_weight.shape[2:4]
        nb = slots // bs
        nh = send_list.shape[3]
        nr = remap_weight.shape[1]
        nf = flux_weight.shape[1]
        natm = secs - 1
        nba = nb // 2
        f32, bf16 = jnp.float32, jnp.bfloat16
        hbm = pl.BlockSpec(memory_space=pl.ANY)
        smem = pl.BlockSpec(memory_space=pltpu.SMEM)
        vmem = pl.BlockSpec(memory_space=pltpu.VMEM)
        dma = pltpu.SemaphoreType.DMA
        return pl.pallas_call(
            functools.partial(kernel, secs, doms),
            out_shape=jax.ShapeDtypeStruct(state.shape, f32),
            in_specs=[hbm, smem, smem, hbm, vmem, vmem, smem, hbm, vmem],
            out_specs=hbm,
            scratch_shapes=[
                pltpu.VMEM((STEPS + 1, nb, levels, bs), f32),
                pltpu.VMEM((nb + 2 * nh, 2 * levels, bs), bf16),
                pltpu.VMEM((nb, nk * bs, bs), f32),
                pltpu.VMEM((nb, nk * bs, 2 * bs), bf16),
                pltpu.VMEM((nb, nr * bs, bs), f32),
                pltpu.VMEM((nb, nr * bs, 2 * bs), bf16),
                pltpu.VMEM((nb // 2, 3 * levels, 2 * bs), bf16),
                pltpu.VMEM((STEPS, 2, nh, levels, bs), f32),
                pltpu.VMEM((STEPS, 2, nh, levels, bs), f32),
                pltpu.VMEM((STEPS, nba, nf, bs), f32),
                pltpu.VMEM((STEPS, natm - 1, nba, nf, bs), f32),
                pltpu.VMEM((3, natm, nba, nf, bs), f32),
                pltpu.VMEM((3, natm, nba, nf, bs), f32),
                dma,
                dma((WCH,)),
                dma,
                dma,
                dma((STEPS, 2, 2)),
                dma((STEPS, 2, 2)),
                dma((STEPS, FCH)),
                dma((STEPS, natm - 1, FCH)),
                dma((STEPS, natm, FCH, 3)),
                dma((STEPS, natm, FCH, 3)),
            ],
            compiler_params=pltpu.CompilerParams(
                collective_id=0, has_side_effects=True, vmem_limit_bytes=66 * 1000 * 1000
            ),
        )(
            state,
            send_list,
            op_index.transpose(2, 0, 1),
            op_weight.reshape(nb, nk * bs, bs),
            vertical,
            flux_weight,
            remap_index.T,
            remap_weight.reshape(nb, nr * bs, bs),
            wet_mask.reshape(nb, bs),
        )

    in_specs = (
        P("sec", None, "dom"),
        P("sec", "dom", None, None),
        P("sec", "dom", None),
        P("sec", "dom", None, None, None),
        P("sec", None, None),
        P("sec", None, None),
        P("dom", None),
        P("dom", None, None, None),
        P("dom"),
    )
    return jax.shard_map(
        local, mesh=mesh, in_specs=in_specs, out_specs=P("sec", None, "dom"), check_vma=False
    )
```

time: 85.7 us -> 75.9 us (0.89)
  Pallas kernels: 82.9 us -> 73.1 us
    pallas_call x1, Pallas kernels: 82.9 us -> 73.1 us  [local(): pl.pallas_call(functools.partial(kernel, secs, doms), out_shape=jax.Shape...]
where the time goes in v2:
time: 75.9 us; the launch traced here: 75.7 us
  Pallas kernels  73.1 us (96%)
  local copies, waits for them, and re-layouts  2.66 us (4%)
    pallas_call x1, Pallas kernels, local(): pl.pallas_call(functools.partial(kernel, secs, doms), out_shape=jax.Shape...  73.1 us
    unnamed x1, local copies, waits for them, and re-layouts  2.66 us

profile of v2, /device:TPU:3, one launch (start us, length us, event | category | flops | bytes accessed | tf_op | source)
XLA Modules:
  0.0 75.7 jit_solution(3923893629161603898)
XLA Ops:
  0.0 73.1 %shard_map.91 = f32[1,64,6144]{2,1,0:T(8,128)} custom-call(f32[1,64,6144]{2,1,0:T(8,128)} %state.1, s32[1,1,2,12]{3,2,1,0:T(2,128)} %send_list.1, s32[3,1,48]{2,1,0:T(1,128)} %bitcast.8, f32[48,384,128]{2,1,0:T(8,128)} %bitcast.5, f32[1,64,64]{2,1,0:T(8,128)} %vertical.1, f32[1,16,16]{2,1,0:T(8,128)} %flux_weight.1, s32[2,48]{1,0:T(2,128)} %bitcast.9, ...), custom_call_target="tpu_custom_call" | custom-call | tf_op jit(solution)/shard_map/pallas_call | solution.py:416
  73.1 2.7 %copy.11 = f32[1,64,6144]{2,1,0:T(8,128)} copy(f32[1,64,6144]{2,1,0:T(8,128)} %shard_map.91) | data formatting | bytes 3145728

commit v3 on v2

--- a/solution.py
+++ b/solution.py
@@ -163,6 +163,12 @@
             device_id_type=MESH,
         )
 
+    def pass_on(step, c):
+        for s in range(hub):
+            flux(step, s, c).wait_recv()
+            for o, d in around:
+                forward(step, s, c, o, d).start()
+
     def send_halo(step, cur, part):
         for to_next in (True, False):
             j = 1 if to_next else 0
@@ -314,14 +320,10 @@
             def _():
                 for o, d in around:
                     forward(step, hub, c, o, d).start()
-
-        @pl.when(is_hub)
-        def _():
-            for c in range(FCH):
-                for s in range(hub):
-                    flux(step, s, c).wait_recv()
-                    for o, d in around:
-                        forward(step, s, c, o, d).start()
+                if last:
+                    pass_on(step, c)
+                elif c > 0:
+                    pass_on(step, c - 1)
 
         @pl.when(jnp.logical_not(is_ocean))
         def _():
@@ -331,6 +333,11 @@
                 else:
                     send_halo(step + 1, new, part)
             if not last:
+
+                @pl.when(is_hub)
+                def _():
+                    pass_on(step, FCH - 1)
+
                 for part in range(2):
                     split_own(new, part)
 

time: 75.9 us -> 74.1 us (0.976)
  Pallas kernels: 73.1 us -> 71.2 us
    pallas_call x1, Pallas kernels: 73.1 us -> 71.2 us  [local(): pl.pallas_call(functools.partial(kernel, secs, doms), out_shape=jax.Shape...]
where the time goes in v3:
time: 74.1 us; the launch traced here: 73.9 us
  Pallas kernels  71.2 us (96%)
  local copies, waits for them, and re-layouts  2.66 us (4%)
    pallas_call x1, Pallas kernels, local(): pl.pallas_call(functools.partial(kernel, secs, doms), out_shape=jax.Shape...  71.2 us
    unnamed x1, local copies, waits for them, and re-layouts  2.66 us

profile of v3, /device:TPU:3, one launch (start us, length us, event | category | flops | bytes accessed | tf_op | source)
XLA Modules:
  0.0 73.9 jit_solution(2697504756925063877)
XLA Ops:
  0.0 71.2 %shard_map.91 = f32[1,64,6144]{2,1,0:T(8,128)} custom-call(f32[1,64,6144]{2,1,0:T(8,128)} %state.1, s32[1,1,2,12]{3,2,1,0:T(2,128)} %send_list.1, s32[3,1,48]{2,1,0:T(1,128)} %bitcast.8, f32[48,384,128]{2,1,0:T(8,128)} %bitcast.5, f32[1,64,64]{2,1,0:T(8,128)} %vertical.1, f32[1,16,16]{2,1,0:T(8,128)} %flux_weight.1, s32[2,48]{1,0:T(2,128)} %bitcast.9, ...), custom_call_target="tpu_custom_call" | custom-call | tf_op jit(solution)/shard_map/pallas_call | solution.py:423
  71.2 2.7 %copy.11 = f32[1,64,6144]{2,1,0:T(8,128)} copy(f32[1,64,6144]{2,1,0:T(8,128)} %shard_map.91) | data formatting | bytes 3145728
